TPU v7x, 32 devices: a whole 2x2x4 slice. The times are simulated.
32 devices in a mesh: wide: 8 (over y, x, core), narrow: 4 (over z).
Axes of the slice: x: 2, y: 2, z: 4, core: 2. Of those that a mesh axis runs over, the one named last changes fastest.
Arguments:
- pooled: bfloat16 [16384, 1024], P(('wide', 'narrow')), may hold values from -6 to 6
- cotangent: bfloat16 [16384, 512], P(('wide', 'narrow')), may hold values from -6 to 6
- w_first: bfloat16 [1024, 1024], P('narrow'), may hold values from -0.1875 to 0.1875
- b_first: float32 [1024], replicated, may hold values from -5 to 5
- w_second: bfloat16 [1024, 512], P('narrow'), may hold values from -0.1875 to 0.1875
- counts: bfloat16 [8, 64, 16384], P(None, 'narrow', 'wide'), may hold values from 0 to 3, as said below
- row_ids: int32 [8, 64], P(None, 'narrow'), may hold values from 0 to 63, as said below
- table: float32 [8, 256, 128], P(None, 'narrow'), may hold values from -6 to 6
- accum: float32 [8, 256, 128], P(None, 'narrow'), may hold values from 0.1 to 10
Outputs:
- new_table: float32 [8, 256, 128], P(None, 'narrow')
- new_accum: float32 [8, 256, 128], P(None, 'narrow')
Inputs may be any that keep to these rules, and one draw needn't show every extreme that they name: `counts`: each entry is zero where the sample does not look up the active row, else a positive lookup weight. `row_ids`: for each table, the 16 ids of one owner (slots j * 16 to (j + 1) * 16 - 1) are distinct.
All inputs are finite; a program needn't handle non-finite values.
Results may differ from a plain program's by a relative error of at most 0.0038.
Values may be sent and summed in bfloat16 or wider, within the bound.
A program may use at most 128 MiB of HBM per device.

v0:
```python
import math
import jax
import jax.numpy as jnp
from jax import lax
from jax.sharding import PartitionSpec as P

clip_factor = 0.5
learn_rate = 0.05
epsilon = 1e-08


def tower_back(inputs, cotangent, w_first, b_first, w_second):
    hidden_in = jnp.dot(inputs, w_first, preferred_element_type=jnp.float32) + b_first
    back_hidden = lax.dot_general(
        cotangent, w_second, (((1,), (1,)), ((), ())), preferred_element_type=jnp.float32
    )
    sigmoid_val = jax.nn.sigmoid(hidden_in)
    slopes = sigmoid_val * (1.0 + hidden_in * (1.0 - sigmoid_val))
    deltas = (back_hidden * slopes).astype(jnp.bfloat16)
    return lax.dot_general(
        deltas, w_first, (((1,), (1,)), ((), ())), preferred_element_type=jnp.float32
    ).astype(jnp.bfloat16)


def clip_rows(grads, limit):
    norms = jnp.sqrt(jnp.sum(grads * grads, axis=-1, keepdims=True))
    return grads * (limit / jnp.maximum(norms, limit))


def adagrad_rows(current, old_acc, summed):
    new_acc = old_acc + summed * summed
    return (current - learn_rate * summed / (jnp.sqrt(new_acc) + epsilon), new_acc)


def shards(pooled, cotangent, w_first, b_first, w_second, counts, row_ids, table, accum):
    full_first, full_second = (
        lax.all_gather(w_first, "narrow", axis=0, tiled=True),
        lax.all_gather(w_second, "narrow", axis=0, tiled=True),
    )
    grad_in = tower_back(pooled, cotangent, full_first, b_first, full_second)
    tables = counts.shape[0]
    slots = counts.shape[1]
    bags = counts.shape[2]
    emb = table.shape[2]
    samples = pooled.shape[0]
    scale = 1.0 / math.sqrt(bags)
    limit = clip_factor * math.sqrt(emb)
    regrouped = lax.all_to_all(counts, "narrow", split_axis=2, concat_axis=1, tiled=True)
    local_grad = grad_in.reshape(samples, tables, emb)
    grads = lax.psum_scatter(
        jnp.einsum(
            "tab,btd->atd", regrouped, local_grad, preferred_element_type=jnp.float32
        ).reshape(slots * lax.axis_size("narrow"), tables * emb),
        "narrow",
        scatter_dimension=0,
        tiled=True,
    ).reshape(slots, tables, emb)
    clipped = clip_rows(grads * scale, limit)
    table_index = jnp.arange(tables, dtype=jnp.int32)[:, None]
    current = jnp.transpose(table[table_index, row_ids], (1, 0, 2))
    old_acc = jnp.transpose(accum[table_index, row_ids], (1, 0, 2))
    summed = lax.psum(clipped, "wide")
    new_rows, new_acc = adagrad_rows(current, old_acc, summed)
    new_table = table.at[table_index, row_ids].set(jnp.transpose(new_rows, (1, 0, 2)))
    new_accum = accum.at[table_index, row_ids].set(jnp.transpose(new_acc, (1, 0, 2)))
    return (new_table, new_accum)


def solution(mesh):
    in_specs = (
        P(("wide", "narrow"), None),
        P(("wide", "narrow"), None),
        P("narrow", None),
        P(),
        P("narrow", None),
        P(None, "narrow", "wide"),
        P(None, "narrow"),
        P(None, "narrow", None),
        P(None, "narrow", None),
    )
    out_specs = (P(None, "narrow", None), P(None, "narrow", None))
    return jax.shard_map(shards, mesh=mesh, in_specs=in_specs, out_specs=out_specs, check_vma=False)
```

profile of v0, /device:TPU:0, one launch (start us, length us, event | category | flops | bytes accessed | tf_op | source)
XLA Modules:
  0.0 199.6 jit_solution(9209073839710677612)
XLA Ops:
  7.2 1.1 copy.53
  8.3 0.9 copy.54
  9.3 0.7 all-gather.3.cloned.1.call-update
  10.1 4.2 %copy.26 = bf16[8,16,2048]{1,0,2:T(8,128)(2,1)} copy(bf16[8,16,2048]{2,1,0:T(8,128)(2,1)S(1)} %copy-done.3) | data formatting | bytes 1048576 | tf_op args[5]
  14.3 5.8 %reshape.51 = bf16[4,2,32768]{2,1,0:T(2,128)(2,1)S(1)} reshape(bf16[2048,8,16]{2,1,0:T(8,128)(2,1)} %bitcast.58) | data formatting | bytes 1048576
  20.1 35.4 %all_to_all.18 = bf16[4,2,32768]{2,1,0:T(2,128)(2,1)S(1)} all-to-all(bf16[4,2,32768]{2,1,0:T(2,128)(2,1)S(1)} %reshape.51), channel_id=1, replica_groups=mesh['wide'=8,'narrow'=4] {'narrow'}, dimensions={0} | all-to-all | bytes 1048576 | tf_op jit(solution)/shard_map/all_to_all | solution.py:48
  55.5 4.1 %reshape.52 = bf16[2048,8,16]{2,1,0:T(8,128)(2,1)} reshape(bf16[4,2,32768]{2,1,0:T(2,128)(2,1)S(1)} %all_to_all.18) | data formatting | bytes 1048576
  59.7 4.4 %copy.27 = bf16[8,16,4,512]{3,1,2,0:T(8,128)(2,1)S(1)} copy(bf16[8,16,4,512]{1,0,3,2:T(8,128)(2,1)} %bitcast.57) | data formatting | bytes 1048576 | tf_op jit(solution)/shard_map/all_to_all | solution.py:48
  64.1 5.2 %all-gather.5.cloned.1.call-done = bf16[1024,1024]{1,0:T(8,128)(2,1)} async-done(((bf16[256,1024]{1,0:T(8,128)(2,1)}), bf16[1024,1024]{1,0:T(8,128)(2,1)}) %all-gather.5.cloned.1.call-update) | async-done | bytes 2097168 | tf_op jit(solution)/shard_map/all_gather | solution.py:37
  69.2 4.2 %fusion.13 = f32[512,1024]{1,0:T(8,128)} fusion(bf16[512,1024]{1,0:T(8,128)(2,1)S(1)} %copy-done, bf16[1024,1024]{1,0:T(8,128)(2,1)} %all-gather.5.cloned.1.call-done), kind=kOutput, calls=%fused_computation.32 | convolution fusion | flops 1073741824 | bytes 5242880 | tf_op jit(solution)/shard_map/dot_general | solution.py:13
  73.4 24.1 %all-gather.3.cloned.1.call-done = bf16[1024,512]{1,0:T(8,128)(2,1)} async-done(((bf16[256,512]{1,0:T(8,128)(2,1)}), bf16[1024,512]{1,0:T(8,128)(2,1)}) %all-gather.3.cloned.1.call-update) | async-done | bytes 1048592 | tf_op jit(solution)/shard_map/all_gather | solution.py:38
  97.5 4.6 %fusion = bf16[64,8,8,128]{3,2,1,0:T(8,128)(2,1)S(1)} fusion(bf16[1024,1024]{1,0:T(8,128)(2,1)} %all-gather.5.cloned.1.call-done, f32[512,1024]{1,0:T(8,128)} %fusion.13, bf16[512,512]{1,0:T(8,128)(2,1)} %param.10, bf16[1024,512]{1,0:T(8,128)(2,1)} %all-gather.3.cloned.1.call-done, f32[1024]{0:T(1024)S(1)} %copy-done.5), kind=kOutput, calls=%fused_computation.6 | convolution fusion | flops 1616379904 | bytes 6819840 | tf_op jit(solution)/shard_map/dot_general | solution.py:20
  102.1 0.3 convolution_bitcast_fusion
  102.4 0.7 copy.47
  103.2 19.5 %reduce-scatter.2.cloned.1.call-done = f32[16,1024]{1,0:T(8,128)} async-done(((f32[64,1024]{1,0:T(8,128)}), f32[16,1024]{1,0:T(8,128)}) %reduce-scatter.2.cloned.1.call-update) | async-done | bytes 65552 | tf_op jit(solution)/shard_map/reduce_scatter | solution.py:50
  122.7 0.9 copy.35
  123.7 0.7 bitcast_multiply_fusion
  124.5 1.2 gather_fusion
  125.7 1.2 gather_fusion.1
  127.1 50.5 %all-reduce.2.cloned.1.call-done = f32[16,8,128]{2,1,0:T(8,128)} async-done(((f32[16,8,128]{2,1,0:T(8,128)}), f32[16,8,128]{2,1,0:T(8,128)}) %all-reduce.2.cloned.1.call-update) | async-done | bytes 65552 | tf_op jit(solution)/shard_map/psum | solution.py:62
  177.6 0.9 fusion.6
  178.6 6.9 %scatter_fusion.1 = f32[8,64,128]{2,1,0:T(8,128)S(1)} fusion(f32[8,64,128]{2,1,0:T(8,128)S(1)} %copy.54, s32[128]{0:T(128)S(1)} %reshape.39, f32[128,128]{1,0:T(8,128)S(1)} %bitcast.64), kind=kCustom, calls=%fused_computation.3 | custom fusion | bytes 197632 | tf_op jit(solution)/shard_map/scatter | solution.py:65
  185.5 6.9 %scatter_fusion = f32[8,64,128]{2,1,0:T(8,128)S(1)} fusion(f32[8,64,128]{2,1,0:T(8,128)S(1)} %copy.53, s32[128]{0:T(128)S(1)} %reshape.39, f32[128,128]{1,0:T(8,128)S(1)} %bitcast.63), kind=kCustom, calls=%fused_computation.2 | custom fusion | bytes 197632 | tf_op jit(solution)/shard_map/scatter | solution.py:64
  192.4 0.7 copy-done.1
  (26 shorter events, 0.5 us)
Async XLA Ops:
  7.2 62.1 %copy-start = (bf16[512,1024]{1,0:T(8,128)(2,1)S(1)}, bf16[512,1024]{1,0:T(8,128)(2,1)}, u32[]{:S(2)}) copy-start(bf16[512,1024]{1,0:T(8,128)(2,1)} %param.9) | copy-start | bytes 3145732
  7.2 2.9 %copy-start.3 = (bf16[8,16,2048]{2,1,0:T(8,128)(2,1)S(1)}, bf16[8,16,2048]{2,1,0:T(8,128)(2,1)}, u32[]{:S(2)}) copy-start(bf16[8,16,2048]{2,1,0:T(8,128)(2,1)} %param.14) | copy-start | bytes 1572868
  7.2 62.0 %all-gather.5.cloned.1.call-start = ((), (), s32[]{:S(2)}) async-start(), calls=%async_computation.3 | async-start | bytes 2621440 | tf_op jit(solution)/shard_map/all_gather | solution.py:37
  9.3 88.2 %all-gather.3.cloned.1.call-start = ((), (), s32[]{:S(2)}) async-start(), calls=%async_computation.2 | async-start | bytes 1310720 | tf_op jit(solution)/shard_map/all_gather | solution.py:38
  10.0 112.6 %reduce-scatter.2.cloned.1.call-start = ((), (), s32[]{:S(2)}) async-start(), calls=%async_computation.4 | async-start | bytes 327680 | tf_op jit(solution)/shard_map/reduce_scatter | solution.py:50
  64.1 33.4 %copy-start.5 = (f32[1024]{0:T(1024)S(1)}, f32[1024]{0:T(1024)}, u32[]{:S(2)}) copy-start(f32[1024]{0:T(1024)} %param.12) | copy-start | bytes 12292
  102.0 22.4 %copy-start.4 = (s32[8,16]{1,0:T(8,128)S(1)}, s32[8,16]{1,0:T(8,128)}, u32[]{:S(2)}) copy-start(s32[8,16]{1,0:T(8,128)} %param.15) | copy-start | bytes 1540
  103.1 74.5 %all-reduce.2.cloned.1.call-start = ((), (), s32[]{:S(2)}) async-start(), calls=%async_computation.5 | async-start | bytes 131072 | tf_op jit(solution)/shard_map/psum | solution.py:62
  185.5 6.9 %copy-start.2 = (f32[8,64,128]{2,1,0:T(8,128)}, f32[8,64,128]{2,1,0:T(8,128)S(1)}, u32[]{:S(2)}) copy-start(f32[8,64,128]{2,1,0:T(8,128)S(1)} %scatter_fusion.1) | copy-start | bytes 786436
  192.4 0.7 copy-start.1
Sparse Core Ops, SparseCore 0:
  9.6 59.6 all-gather.4
  70.8 26.6 all-gather.2
  103.3 19.3 reduce-scatter.1
  126.2 51.3 all-reduce.1
where the time goes:
time: 200 us
  waiting for transfers between devices  100 us (50%)
  local copies, waits for them, and re-layouts  39.3 us (20%)
  blocking collectives  35.4 us (18%)
  between operations  13.9 us (7%)
  matrix products  9.06 us (5%)
    psum x1, waiting for transfers between devices, shards(): summed = lax.psum(clipped, 'wide')  50.5 us
    all_to_all x1, blocking collectives, shards(): lax.all_to_all(counts, 'narrow', split_axis=2, concat_axis=1, tiled=True)  35.4 us
    all_gather x1, waiting for transfers between devices, shards(): lax.all_gather(w_second, 'narrow', axis=0, tiled=True)  24.1 us
    reduce_scatter x1, waiting for transfers between devices, shards(): lax.psum_scatter(jnp.einsum('tab,btd->atd', regrouped, local_grad, prefer...  19.5 us
    unnamed x18, local copies, waits for them, and re-layouts  17.7 us
    scatter x1, local copies, waits for them, and re-layouts, shards(): accum.at[table_index, row_ids].set(jnp.transpose(new_acc, (1, 0, 2)))  6.9 us
    scatter x1, local copies, waits for them, and re-layouts, shards(): table.at[table_index, row_ids].set(jnp.transpose(new_rows, (1, 0, 2)))  6.9 us
    all_gather x1, waiting for transfers between devices, shards(): lax.all_gather(w_first, 'narrow', axis=0, tiled=True)  5.15 us
  transfers between devices with their start and end apart: 4, of which 4 were waited for; matrix products, arithmetic and copies ran while one was open for 13% of the time, Pallas kernels for 0%

commit v1 on v0

--- a/solution.py
+++ b/solution.py
@@ -45,7 +45,16 @@
     samples = pooled.shape[0]
     scale = 1.0 / math.sqrt(bags)
     limit = clip_factor * math.sqrt(emb)
-    regrouped = lax.all_to_all(counts, "narrow", split_axis=2, concat_axis=1, tiled=True)
+    _treat_ports = lambda piece_in: jnp.concatenate(
+        lax.all_to_all(
+            jnp.stack(jnp.split(piece_in, lax.psum(1, axis_name="narrow"), 2), 0),
+            axis_name="narrow",
+            split_axis=0,
+            concat_axis=0,
+        ),
+        1,
+    )
+    regrouped = _treat_ports(counts)
     local_grad = grad_in.reshape(samples, tables, emb)
     grads = lax.psum_scatter(
         jnp.einsum(

time: 200 us -> 196 us (0.980)
  local copies, waits for them, and re-layouts: 39.3 us -> 20.9 us
  waiting for transfers between devices: 100 us -> 118 us
  blocking collectives: 35.4 us -> 32.5 us
    all_gather x1, waiting for transfers between devices: 5.15 us -> 22.4 us  [shards(): lax.all_gather(w_first, 'narrow', axis=0, tiled=True)]
    unnamed x18 -> x15, local copies, waits for them, and re-layouts: 17.7 us -> 3.61 us
    all_to_all x1 -> x0, local copies, waits for them, and re-layouts: 4.4 us -> none  [shards(): lax.all_to_all(counts, 'narrow', split_axis=2, concat_axis=1, tiled=True)]
    all_to_all x1, blocking collectives: 35.4 us -> 32.5 us  [shards(): lax.all_to_all(jnp.stack(jnp.split(piece_in, lax.psum(1, axis_name='narro...]
  transfers between devices with their start and end apart: 4 -> 4, of which waited for: 4 -> 4; matrix products, arithmetic and copies ran while one was open for 13% -> 4% of each run, Pallas kernels for 0% -> 0%
where the time goes in v1:
time: 196 us
  waiting for transfers between devices  118 us (60%)
  blocking collectives  32.5 us (17%)
  local copies, waits for them, and re-layouts  20.9 us (11%)
  between operations  13.9 us (7%)
  matrix products  9.02 us (5%)
    psum x1, waiting for transfers between devices, shards(): summed = lax.psum(clipped, 'wide')  50.6 us
    all_to_all x1, blocking collectives, shards(): lax.all_to_all(jnp.stack(jnp.split(piece_in, lax.psum(1, axis_name='narro...  32.5 us
    all_gather x1, waiting for transfers between devices, shards(): lax.all_gather(w_second, 'narrow', axis=0, tiled=True)  24.5 us
    all_gather x1, waiting for transfers between devices, shards(): lax.all_gather(w_first, 'narrow', axis=0, tiled=True)  22.4 us
    reduce_scatter x1, waiting for transfers between devices, shards(): lax.psum_scatter(jnp.einsum('tab,btd->atd', regrouped, local_grad, prefer...  19.5 us
    scatter x1, local copies, waits for them, and re-layouts, shards(): table.at[table_index, row_ids].set(jnp.transpose(new_rows, (1, 0, 2)))  6.9 us
    scatter x1, local copies, waits for them, and re-layouts, shards(): accum.at[table_index, row_ids].set(jnp.transpose(new_acc, (1, 0, 2)))  6.9 us
    dot_general x1, matrix products, tower_back(): lax.dot_general(deltas, w_first, (((1,), (1,)), ((), ())), preferred_elem...  4.55 us
  transfers between devices with their start and end apart: 4, of which 4 were waited for; matrix products, arithmetic and copies ran while one was open for 4% of the time, Pallas kernels for 0%

profile of v1, /device:TPU:0, one launch (start us, length us, event | category | flops | bytes accessed | tf_op | source)
XLA Modules:
  0.0 196.0 jit_solution(15080549410355503688)
XLA Ops:
  7.2 1.1 copy.45
  8.3 0.9 copy.46
  9.3 0.7 all-gather.3.cloned.1.call-update
  10.2 0.1 pad_maximum_fusion
  10.2 32.5 %all_to_all.5 = bf16[4,8,16,512]{3,2,1,0:T(8,128)(2,1)S(1)} all-to-all(bf16[4,8,16,512]{3,2,1,0:T(8,128)(2,1)S(1)} %pad_maximum_fusion), channel_id=1, replica_groups=mesh['wide'=8,'narrow'=4] {'narrow'}, dimensions={0} | all-to-all | bytes 1048576 | tf_op jit(solution)/shard_map/all_to_all | solution.py:49
  42.8 22.4 %all-gather.5.cloned.1.call-done = bf16[1024,1024]{1,0:T(8,128)(2,1)} async-done(((bf16[256,1024]{1,0:T(8,128)(2,1)}), bf16[1024,1024]{1,0:T(8,128)(2,1)}) %all-gather.5.cloned.1.call-update) | async-done | bytes 2097168 | tf_op jit(solution)/shard_map/all_gather | solution.py:37
  65.1 4.1 %fusion.13 = f32[512,1024]{1,0:T(8,128)} fusion(bf16[512,1024]{1,0:T(8,128)(2,1)S(1)} %copy-done, bf16[1024,1024]{1,0:T(8,128)(2,1)} %all-gather.5.cloned.1.call-done), kind=kOutput, calls=%fused_computation.37 | convolution fusion | flops 1073741824 | bytes 5242880 | tf_op jit(solution)/shard_map/dot_general | solution.py:13
  69.3 24.5 %all-gather.3.cloned.1.call-done = bf16[1024,512]{1,0:T(8,128)(2,1)} async-done(((bf16[256,512]{1,0:T(8,128)(2,1)}), bf16[1024,512]{1,0:T(8,128)(2,1)}) %all-gather.3.cloned.1.call-update) | async-done | bytes 1048592 | tf_op jit(solution)/shard_map/all_gather | solution.py:38
  93.8 4.6 %fusion = bf16[64,8,8,128]{3,2,1,0:T(8,128)(2,1)S(1)} fusion(bf16[1024,1024]{1,0:T(8,128)(2,1)} %all-gather.5.cloned.1.call-done, f32[512,1024]{1,0:T(8,128)} %fusion.13, bf16[512,512]{1,0:T(8,128)(2,1)} %param.10, bf16[1024,512]{1,0:T(8,128)(2,1)} %all-gather.3.cloned.1.call-done, f32[1024]{0:T(1024)S(1)} %copy-done.5), kind=kOutput, calls=%fused_computation.6 | convolution fusion | flops 1616379904 | bytes 6819840 | tf_op jit(solution)/shard_map/dot_general | solution.py:20
  98.4 0.3 convolution_bitcast_fusion
  98.7 0.7 copy.39
  99.5 19.5 %reduce-scatter.2.cloned.1.call-done = f32[16,1024]{1,0:T(8,128)} async-done(((f32[64,1024]{1,0:T(8,128)}), f32[16,1024]{1,0:T(8,128)}) %reduce-scatter.2.cloned.1.call-update) | async-done | bytes 65552 | tf_op jit(solution)/shard_map/reduce_scatter | solution.py:59
  119.0 0.9 copy.27
  119.9 0.1 multiply_reduce_fusion
  120.0 0.7 bitcast_multiply_fusion
  120.7 0.1 reshape.35
  120.8 1.2 gather_fusion
  122.1 1.2 gather_fusion.1
  123.3 0.1 reshape.47
  123.4 50.6 %all-reduce.2.cloned.1.call-done = f32[16,8,128]{2,1,0:T(8,128)} async-done(((f32[16,8,128]{2,1,0:T(8,128)}), f32[16,8,128]{2,1,0:T(8,128)}) %all-reduce.2.cloned.1.call-update) | async-done | bytes 65552 | tf_op jit(solution)/shard_map/psum | solution.py:71
  173.9 0.9 fusion.6
  174.9 6.9 %scatter_fusion.1 = f32[8,64,128]{2,1,0:T(8,128)S(1)} fusion(f32[8,64,128]{2,1,0:T(8,128)S(1)} %copy.46, s32[128]{0:T(128)S(1)} %reshape.47, f32[128,128]{1,0:T(8,128)S(1)} %bitcast.67), kind=kCustom, calls=%fused_computation.3 | custom fusion | bytes 197632 | tf_op jit(solution)/shard_map/scatter | solution.py:74
  181.8 6.9 %scatter_fusion = f32[8,64,128]{2,1,0:T(8,128)S(1)} fusion(f32[8,64,128]{2,1,0:T(8,128)S(1)} %copy.45, s32[128]{0:T(128)S(1)} %reshape.47, f32[128,128]{1,0:T(8,128)S(1)} %bitcast.66), kind=kCustom, calls=%fused_computation.2 | custom fusion | bytes 197632 | tf_op jit(solution)/shard_map/scatter | solution.py:73
  188.7 0.7 copy-done.1
  (25 shorter events, 0.4 us)
Async XLA Ops:
  7.2 58.0 %copy-start = (bf16[512,1024]{1,0:T(8,128)(2,1)S(1)}, bf16[512,1024]{1,0:T(8,128)(2,1)}, u32[]{:S(2)}) copy-start(bf16[512,1024]{1,0:T(8,128)(2,1)} %param.9) | copy-start | bytes 3145732
  7.2 2.9 %copy-start.3 = (bf16[8,16,2048]{2,1,0:T(8,128)(2,1)S(1)}, bf16[8,16,2048]{2,1,0:T(8,128)(2,1)}, u32[]{:S(2)}) copy-start(bf16[8,16,2048]{2,1,0:T(8,128)(2,1)} %param.14) | copy-start | bytes 1572868
  7.2 57.9 %all-gather.5.cloned.1.call-start = ((), (), s32[]{:S(2)}) async-start(), calls=%async_computation.3 | async-start | bytes 2621440 | tf_op jit(solution)/shard_map/all_gather | solution.py:37
  9.3 84.5 %all-gather.3.cloned.1.call-start = ((), (), s32[]{:S(2)}) async-start(), calls=%async_computation.2 | async-start | bytes 1310720 | tf_op jit(solution)/shard_map/all_gather | solution.py:38
  10.0 109.0 %reduce-scatter.2.cloned.1.call-start = ((), (), s32[]{:S(2)}) async-start(), calls=%async_computation.4 | async-start | bytes 327680 | tf_op jit(solution)/shard_map/reduce_scatter | solution.py:59
  42.8 51.1 %copy-start.5 = (f32[1024]{0:T(1024)S(1)}, f32[1024]{0:T(1024)}, u32[]{:S(2)}) copy-start(f32[1024]{0:T(1024)} %param.12) | copy-start | bytes 12292
  98.4 22.3 %copy-start.4 = (s32[8,16]{1,0:T(8,128)S(1)}, s32[8,16]{1,0:T(8,128)}, u32[]{:S(2)}) copy-start(s32[8,16]{1,0:T(8,128)} %param.15) | copy-start | bytes 1540
  99.5 74.5 %all-reduce.2.cloned.1.call-start = ((), (), s32[]{:S(2)}) async-start(), calls=%async_computation.5 | async-start | bytes 131072 | tf_op jit(solution)/shard_map/psum | solution.py:71
  181.8 6.9 %copy-start.2 = (f32[8,64,128]{2,1,0:T(8,128)}, f32[8,64,128]{2,1,0:T(8,128)S(1)}, u32[]{:S(2)}) copy-start(f32[8,64,128]{2,1,0:T(8,128)S(1)} %scatter_fusion.1) | copy-start | bytes 786436
  188.7 0.7 copy-start.1
Sparse Core Ops, SparseCore 0:
  9.6 55.5 all-gather.4
  66.7 27.0 all-gather.2
  99.6 19.3 reduce-scatter.1
  122.5 51.4 all-reduce.1
